TPU v7x, 32 devices: a whole 2x2x4 slice. The times are simulated.
32 devices in a mesh: blk: 16 (over z, x, core), feat: 2 (over y).
Axes of the slice: x: 2, y: 2, z: 4, core: 2. Of those that a mesh axis runs over, the one named last changes fastest.
Arguments:
- inputs: bfloat16 [4096, 1024], P('blk'), may hold values from -6 to 6
- col_mask: int32 [2, 1024], replicated, may hold values 0 or 1
- row_mask: int32 [4096], P('blk'), may hold values from 0 to 1
- width_class: int32 [4096], P('blk'), may hold values from 0 to 1
- frequencies: bfloat16 [2048, 2048], P(None, 'feat'), may hold values from -0.375 to 0.375
- phases: float32 [2048], P('feat'), may hold values from -3.140625 to 3.140625
- targets: float32 [4096], P('blk'), may hold values from -6 to 6
- prior_draws: float32 [4096, 16], P('blk'), may hold values from -6 to 6
- hidden_weight: float32 [1024, 2048], P('blk', 'feat'), may hold values from -0.1875 to 0.1875
- hidden_moment: float32 [1024, 2048], P('blk', 'feat'), may hold values from -9.536743e-06 to 9.536743e-06
- hidden_second: float32 [1024, 2048], P('blk', 'feat'), may hold values from 4.2e-14 to 1.7e-13
- alpha_weight: float32 [4096, 16], P('blk'), may hold values from -1.5 to 1.5
- alpha_moment: float32 [4096, 16], P('blk'), may hold values from -2.2888184e-05 to 2.2888184e-05
- alpha_second: float32 [4096, 16], P('blk'), may hold values from 1.7578125e-13 to 7.080078e-13
Outputs:
- norm_before: float32 [], replicated
- resid_norm: float32 [], replicated
- hidden_out: float32 [1024, 2048], P('blk', 'feat')
- hidden_moment_out: float32 [1024, 2048], P('blk', 'feat')
- hidden_second_out: float32 [1024, 2048], P('blk', 'feat')
- hidden_copy: bfloat16 [1024, 2048], P('blk', 'feat')
- alpha_out: float32 [4096, 16], P('blk')
- alpha_moment_out: float32 [4096, 16], P('blk')
- alpha_second_out: float32 [4096, 16], P('blk')
- alpha_copy: bfloat16 [4096, 16], P('blk')
All inputs are finite; a program needn't handle non-finite values.
Results may differ from a plain program's by a relative error of at most 0.0034.
Values may be sent and summed in bfloat16 or wider, within the bound.
No kernel may reach another device: no remote copies, remote signals or barrier semaphores. Data moves between devices by JAX's collectives and lax.ppermute only.
A program may use at most 192 MiB of HBM per device.

v0:
```python
import jax
import jax.numpy as jnp
from jax import lax
from jax.sharding import PartitionSpec as P

F = 2048
S = 16
ADAM_STEP = 10
PRECISE = lax.Precision.HIGHEST
NOISE = 0.01
CLIP_AT = 0.01
BETA_ONE = 0.9
BETA_TWO = 0.999
ADAM_EPS = 1e-08
DECAY = 0.01


def adamw_update(weight, moment, second, gradient, step_rate):
    moment = BETA_ONE * moment + (1.0 - BETA_ONE) * gradient
    second = BETA_TWO * second + (1.0 - BETA_TWO) * gradient * gradient
    moment_hat = moment / (1.0 - BETA_ONE**ADAM_STEP)
    second_hat = second / (1.0 - BETA_TWO**ADAM_STEP)
    weight = weight - step_rate * (moment_hat / (jnp.sqrt(second_hat) + ADAM_EPS) + DECAY * weight)
    return (weight, moment, second)


def kernel_step(features, pieces):
    kernel = jnp.einsum("tf,pf->tp", features, pieces[0], preferred_element_type=jnp.float32)
    fitted = jnp.dot(kernel, pieces[1].astype(jnp.float32), precision=PRECISE)
    summed = jnp.einsum("pf,ps->fs", pieces[0], pieces[1], preferred_element_type=jnp.float32)
    return (fitted, summed)


def on_device(
    inputs,
    col_mask,
    row_mask,
    width_class,
    frequencies,
    phases,
    targets,
    prior_draws,
    hidden_weight,
    hidden_moment,
    hidden_second,
    alpha_weight,
    alpha_moment,
    alpha_second,
):
    classes = col_mask.shape[0]
    feat_scale = (2.0 / F) ** 0.5
    onehot = (width_class[:, None] == jnp.arange(classes, dtype=jnp.int32)[None, :]).astype(
        jnp.float32
    )
    keep_cols = jnp.dot(onehot, col_mask.astype(jnp.float32))
    masked = inputs * keep_cols.astype(jnp.bfloat16)
    keep_rows = row_mask.astype(jnp.float32)
    true_count = jnp.maximum(lax.psum(jnp.sum(keep_rows), "blk"), 1.0)
    columns = masked
    first_pre = jnp.dot(
        columns,
        lax.all_gather(hidden_weight.astype(jnp.bfloat16), "blk", axis=0, tiled=True),
        preferred_element_type=jnp.float32,
    )
    tanh_full = jnp.tanh(first_pre)
    hidden = tanh_full.astype(jnp.bfloat16)
    pre = jnp.dot(
        lax.all_gather(hidden, "feat", axis=1, tiled=True),
        frequencies,
        preferred_element_type=jnp.float32,
    )
    phase_arg = pre + phases[None, :]
    features = (feat_scale * jnp.cos(phase_arg)).astype(jnp.bfloat16)
    alpha_low = alpha_weight.astype(jnp.bfloat16)

    def fold_step(pieces):
        return kernel_step(features, pieces)

    fitted_part, moments = fold_step(
        (
            lax.all_gather(features, "blk", axis=0, tiled=True),
            lax.all_gather(alpha_low, "blk", axis=0, tiled=True),
        )
    )
    fitted = lax.psum(fitted_part, "feat") + NOISE * alpha_weight
    residual = fitted - targets[:, None] - prior_draws
    resid_grad = (2.0 * keep_rows[:, None] * residual / (true_count * S)).astype(jnp.bfloat16)
    pulled_part, back_moments = fold_step(
        (
            lax.all_gather(features, "blk", axis=0, tiled=True),
            lax.all_gather(resid_grad, "blk", axis=0, tiled=True),
        )
    )
    alpha_grad = lax.psum(pulled_part, "feat") + NOISE * resid_grad.astype(jnp.float32)
    feature_grad = jnp.dot(resid_grad.astype(jnp.float32), moments.T, precision=PRECISE)
    feature_grad = feature_grad + jnp.dot(
        alpha_low.astype(jnp.float32), back_moments.T, precision=PRECISE
    )
    pre_grad = (-feat_scale * jnp.sin(phase_arg) * feature_grad).astype(jnp.bfloat16)
    hidden_terms = jnp.einsum(
        "tf,hf->th", pre_grad, frequencies, preferred_element_type=jnp.float32
    )
    hidden_grad = lax.psum_scatter(hidden_terms, "feat", scatter_dimension=1, tiled=True)
    first_grad = ((1.0 - tanh_full * tanh_full) * hidden_grad).astype(jnp.bfloat16)
    columns = masked
    weight_grad = lax.psum_scatter(
        jnp.einsum("td,th->dh", columns, first_grad, preferred_element_type=jnp.float32),
        "blk",
        scatter_dimension=0,
        tiled=True,
    )
    first_feat = (lax.axis_index("feat") == 0).astype(jnp.float32)
    grad_part = jnp.sum(weight_grad * weight_grad) + first_feat * jnp.sum(alpha_grad * alpha_grad)
    resid_part = first_feat * jnp.sum(keep_rows[:, None] * residual * residual)
    grad_total, resid_total = lax.psum((grad_part, resid_part), ("blk", "feat"))
    norm_before = jnp.sqrt(grad_total)
    resid_norm = jnp.sqrt(resid_total)
    clip = jnp.minimum(1.0, CLIP_AT / (norm_before + 1e-06))
    hidden_out, moment_out, second_out = adamw_update(
        hidden_weight, hidden_moment, hidden_second, weight_grad * clip, 0.02
    )
    alpha_out, alpha_moment_out, alpha_second_out = adamw_update(
        alpha_weight, alpha_moment, alpha_second, alpha_grad * clip, 0.05
    )
    return (
        norm_before,
        resid_norm,
        hidden_out,
        moment_out,
        second_out,
        hidden_out.astype(jnp.bfloat16),
        alpha_out,
        alpha_moment_out,
        alpha_second_out,
        alpha_out.astype(jnp.bfloat16),
    )


def solution(mesh):
    in_specs = (
        P("blk", None),
        P(),
        P("blk"),
        P("blk"),
        P(None, "feat"),
        P("feat"),
        P("blk"),
        P("blk", None),
        P("blk", "feat"),
        P("blk", "feat"),
        P("blk", "feat"),
        P("blk", None),
        P("blk", None),
        P("blk", None),
    )
    out_specs = (
        P(),
        P(),
        P("blk", "feat"),
        P("blk", "feat"),
        P("blk", "feat"),
        P("blk", "feat"),
        P("blk", None),
        P("blk", None),
        P("blk", None),
        P("blk", None),
    )
    return jax.shard_map(
        on_device, mesh=mesh, in_specs=in_specs, out_specs=out_specs, check_vma=False
    )
```

profile of v0, /device:TPU:0, one launch (start us, length us, event | category | flops | bytes accessed | tf_op | source)
XLA Modules:
  0.0 378.5 jit_solution(18336091625798306020)
XLA Ops:
  7.2 0.0 copy-start.11
  7.2 0.0 all-gather.4.cloned.1.call-start
  7.2 1.6 convert_element_type.47
  8.9 0.0 all-gather.4.cloned.1.call-update
  8.9 0.0 all-gather.6.cloned.1.call-start
  8.9 1.4 fusion.3
  10.3 44.6 %all-gather.4.cloned.1.call-done = bf16[1024,1024]{1,0:T(8,128)(2,1)} async-done(((bf16[64,1024]{1,0:T(8,128)(2,1)}), bf16[1024,1024]{1,0:T(8,128)(2,1)}) %all-gather.4.cloned.1.call-update) | async-done | bytes 2097168 | tf_op jit(solution)/shard_map/all_gather | solution.py:62
  54.9 3.1 fusion.16
  58.1 0.0 all-gather.6.cloned.1.call-update
  58.1 0.0 copy-start.8
  58.1 0.0 copy-start.4
  58.1 0.0 all-gather.8.cloned.1.call-start
  58.2 20.1 %all-gather.6.cloned.1.call-done = bf16[256,2048]{1,0:T(8,128)(2,1)} async-done(((bf16[256,1024]{1,0:T(8,128)(2,1)}), bf16[256,2048]{1,0:T(8,128)(2,1)}) %all-gather.6.cloned.1.call-update) | async-done | bytes 1048592 | tf_op jit(solution)/shard_map/all_gather | solution.py:68
  78.3 0.0 copy-done.11
  78.3 7.3 %multiply_convert_fusion.1 = (bf16[256,1024]{1,0:T(8,128)(2,1)}, f32[256,1024]{1,0:T(8,128)S(1)}) fusion(f32[1024]{0:T(1024)S(1)} %copy-done.11, bf16[256,2048]{1,0:T(8,128)(2,1)} %all-gather.6.cloned.1.call-done, bf16[2048,1024]{1,0:T(8,128)(2,1)} %param.18), kind=kOutput, calls=%fused_computation.9 | convolution fusion | flops 1074528256 | bytes 6819840 | tf_op jit(solution)/shard_map/dot_general | solution.py:67
  85.6 0.0 all-gather.8.cloned.1.call-update
  85.6 0.0 reduce-scatter.3.cloned.1.call-start
  85.6 0.0 copy-done.8
  85.6 0.6 broadcast_multiply_fusion
  86.2 34.6 %psum.36 = f32[]{:T(128)} all-reduce(f32[]{:T(128)} %get-tuple-element.23), channel_id=1, replica_groups=mesh['blk'=16,'feat'=2] {'blk'}, use_global_device_ids=true, to_apply=%region_2.0 | all-reduce | flops 1 | bytes 8 | tf_op jit(solution)/shard_map/psum | solution.py:58
  120.8 0.0 copy-done.4
  121.5 18.8 %all_gather.19 = bf16[4096,16]{0,1:T(8,128)(2,1)S(1)} all-gather(bf16[256,16]{0,1:T(8,128)(2,1)S(1)} %convert_element_type.51), channel_id=1, replica_groups=mesh['blk'=16,'feat'=2] {'blk'}, dimensions={0}, use_global_device_ids=true | all-gather | bytes 139264 | tf_op jit(solution)/shard_map/all_gather | solution.py:82
  140.2 20.7 %all-gather.8.cloned.1.call-done = bf16[4096,1024]{1,0:T(8,128)(2,1)} async-done(((bf16[256,1024]{1,0:T(8,128)(2,1)}), bf16[4096,1024]{1,0:T(8,128)(2,1)}) %all-gather.8.cloned.1.call-update) | async-done | bytes 8388624 | tf_op jit(solution)/shard_map/all_gather | solution.py:81
  160.9 5.9 %fusion.17 = f32[256,4096]{1,0:T(8,128)S(1)} fusion(bf16[256,1024]{1,0:T(8,128)(2,1)} %get-tuple-element.26, bf16[4096,1024]{1,0:T(8,128)(2,1)} %all-gather.8.cloned.1.call-done), kind=kOutput, calls=%fused_computation.36 | convolution fusion | flops 2147483648 | bytes 13107200 | tf_op jit(solution)/shard_map/tf,pf->tp/dot_general | solution.py:28
  166.9 0.0 copy-start
  166.9 1.9 copy-done
  168.8 0.0 copy-start.7
  168.8 0.0 copy-start.9
  168.8 2.0 fusion.18
  170.8 8.3 %psum.35 = f32[256,16]{0,1:T(8,128)S(1)} all-reduce(f32[256,16]{0,1:T(8,128)S(1)} %fusion.18), channel_id=1, replica_groups=mesh['blk'=16,'feat'=2] {'feat'}, use_global_device_ids=true, to_apply=%region_0.0 | all-reduce | flops 4096 | bytes 32768 | tf_op jit(solution)/shard_map/psum | solution.py:85
  179.2 0.0 copy-done.7
  179.2 0.0 copy-done.9
  179.2 0.6 fusion.8
  179.8 19.3 %all_gather.20 = bf16[4096,16]{0,1:T(8,128)(2,1)S(1)} all-gather(bf16[256,16]{0,1:T(8,128)(2,1)S(1)} %divide_convert_fusion), channel_id=1, replica_groups=mesh['blk'=16,'feat'=2] {'blk'}, dimensions={0}, use_global_device_ids=true | all-gather | bytes 139264 | tf_op jit(solution)/shard_map/all_gather | solution.py:91
  199.1 5.8 %fusion.19 = f32[1024,16]{1,0:T(8,128)S(1)} fusion(bf16[4096,1024]{1,0:T(8,128)(2,1)} %all-gather.8.cloned.1.call-done, bf16[4096,16]{0,1:T(8,128)(2,1)S(1)} %all_gather.19), kind=kOutput, calls=%fused_computation.38 | convolution fusion | flops 134217728 | bytes 8585216 | tf_op jit(solution)/shard_map/pf,ps->fs/dot_general | solution.py:30
  204.8 0.6 fusion.20
  205.5 0.0 copy-start.10
  205.5 5.9 %fusion.21 = f32[1024,16]{1,0:T(8,128)S(1)} fusion(bf16[4096,1024]{1,0:T(8,128)(2,1)} %all-gather.8.cloned.1.call-done, bf16[4096,16]{0,1:T(8,128)(2,1)S(1)} %all_gather.20), kind=kOutput, calls=%fused_computation.40 | convolution fusion | flops 134217728 | bytes 8585216 | tf_op jit(solution)/shard_map/pf,ps->fs/dot_general | solution.py:30
  211.4 4.3 %fusion.2 = bf16[256,1024]{1,0:T(8,128)(2,1)S(1)} fusion(f32[256,1024]{1,0:T(8,128)S(1)} %fusion.20, f32[1024,16]{1,0:T(8,128)S(1)} %fusion.21, bf16[256,16]{0,1:T(8,128)(2,1)S(1)} %convert_element_type.51, f32[256,1024]{1,0:T(8,128)S(1)} %get-tuple-element.27), kind=kOutput, calls=%fused_computation.5 | convolution fusion | flops 51380224 | bytes 2695168 | tf_op jit(solution)/shard_map/dot_general | solution.py:96
  215.7 0.0 copy-done.10
  215.7 2.6 fusion.22
  218.3 0.0 reduce-scatter.3.cloned.1.call-update
  218.3 0.0 reduce-scatter.5.cloned.1.call-start
  218.4 28.4 %reduce-scatter.3.cloned.1.call-done = f32[256,1024]{1,0:T(8,128)} async-done(((f32[256,2048]{1,0:T(8,128)}), f32[256,1024]{1,0:T(8,128)}) %reduce-scatter.3.cloned.1.call-update) | async-done | bytes 1048592 | tf_op jit(solution)/shard_map/reduce_scatter | solution.py:103
  246.8 3.9 %fusion.4 = f32[1024,1024]{1,0:T(8,128)} fusion(bf16[256,1024]{1,0:T(8,128)(2,1)S(1)} %fusion.3, f32[256,1024]{1,0:T(8,128)} %reduce-scatter.3.cloned.1.call-done, f32[256,1024]{1,0:T(8,128)S(1)} %get-tuple-element.25), kind=kOutput, calls=%fused_computation.10 | convolution fusion | flops 537919488 | bytes 6815744 | tf_op jit(solution)/shard_map/td,th->dh/dot_general | solution.py:107
  250.8 0.0 copy-start.5
  250.8 0.0 copy-start.6
  250.8 0.0 copy-start.1
  250.8 0.0 copy-start.2
  250.8 0.0 copy-start.3
  250.8 0.0 reduce-scatter.5.cloned.1.call-update
  251.5 4.2 %fusion.23 = f32[256,16]{0,1:T(8,128)S(1)} fusion(f32[256,4096]{1,0:T(8,128)} %copy-done, bf16[4096,16]{0,1:T(8,128)(2,1)S(1)} %all_gather.20), kind=kOutput, calls=%fused_computation.42 | convolution fusion | flops 201326592 | bytes 4341760 | tf_op jit(solution)/shard_map/dot_general | solution.py:29
  255.7 7.0 %psum.37 = f32[256,16]{0,1:T(8,128)S(1)} all-reduce(f32[256,16]{0,1:T(8,128)S(1)} %fusion.23), channel_id=1, replica_groups=mesh['blk'=16,'feat'=2] {'feat'}, use_global_device_ids=true, to_apply=%region_6.0 | all-reduce | flops 4096 | bytes 32768 | tf_op jit(solution)/shard_map/psum | solution.py:94
  262.7 0.6 multiply_reduce_fusion.1
  264.0 59.8 %reduce-scatter.5.cloned.1.call-done = f32[64,1024]{1,0:T(8,128)} async-done(((f32[1024,1024]{1,0:T(8,128)}), f32[64,1024]{1,0:T(8,128)}) %reduce-scatter.5.cloned.1.call-update) | async-done | bytes 262160 | tf_op jit(solution)/shard_map/reduce_scatter | solution.py:106
  323.7 1.6 multiply_reduce_fusion
  326.0 39.6 %all-reduce = (f32[]{:T(128)}, f32[]{:T(128)}) all-reduce(f32[]{:T(128)S(6)} %add.72, f32[]{:T(128)S(6)} %mul.177), channel_id=1, replica_groups=mesh['blk'=16,'feat'=2] {'blk','feat'}, use_global_device_ids=true, to_apply=%region_8.0 | all-reduce | flops 2 | bytes 16 | tf_op jit(solution)/shard_map/psum | solution.py:115
  367.0 0.0 copy-done.5
  367.0 0.0 copy-done.6
  367.0 0.6 fusion.12
  367.7 0.0 copy-done.1
  367.7 0.0 copy-done.2
  367.7 0.0 copy-done.3
  367.7 2.0 fusion.14
  (3 shorter events, 0.0 us)
Async XLA Ops:
  7.2 71.1 %copy-start.11 = (f32[1024]{0:T(1024)S(1)}, f32[1024]{0:T(1024)}, u32[]{:S(2)}) copy-start(f32[1024]{0:T(1024)} %param.19) | copy-start | bytes 12292
  7.2 47.8 %all-gather.4.cloned.1.call-start = ((), (), s32[]{:S(2)}) async-start(), calls=%async_computation.2 | async-start | bytes 2228224 | tf_op jit(solution)/shard_map/all_gather | solution.py:62
  8.9 69.4 %all-gather.6.cloned.1.call-start = ((), (), s32[]{:S(2)}) async-start(), calls=%async_computation.3 | async-start | bytes 1572864 | tf_op jit(solution)/shard_map/all_gather | solution.py:68
  58.1 27.5 %copy-start.8 = (s32[256]{0:T(256)S(1)}, s32[256]{0:T(256)}, u32[]{:S(2)}) copy-start(s32[256]{0:T(256)} %param.16) | copy-start | bytes 3076
  58.1 62.7 %copy-start.4 = (f32[256,16]{0,1:T(8,128)S(1)}, f32[256,16]{0,1:T(8,128)}, u32[]{:S(2)}) copy-start(f32[256,16]{0,1:T(8,128)} %param.25) | copy-start | bytes 49156
  58.1 102.8 %all-gather.8.cloned.1.call-start = ((), (), s32[]{:S(2)}) async-start(), calls=%async_computation.4 | async-start | bytes 8912896 | tf_op jit(solution)/shard_map/all_gather | solution.py:81
  85.6 161.2 %reduce-scatter.3.cloned.1.call-start = ((), (), s32[]{:S(2)}) async-start(), calls=%async_computation.5 | async-start | bytes 3145728 | tf_op jit(solution)/shard_map/reduce_scatter | solution.py:103
  166.9 1.9 copy-start
  168.8 10.3 %copy-start.7 = (f32[256,16]{0,1:T(8,128)S(1)}, f32[256,16]{0,1:T(8,128)}, u32[]{:S(2)}) copy-start(f32[256,16]{0,1:T(8,128)} %param.21) | copy-start | bytes 49156
  168.8 10.3 %copy-start.9 = (f32[256]{0:T(256)S(1)}, f32[256]{0:T(256)}, u32[]{:S(2)}) copy-start(f32[256]{0:T(256)} %param.20) | copy-start | bytes 3076
  205.5 10.2 %copy-start.10 = (bf16[2048,1024]{1,0:T(8,128)(2,1)S(1)}, bf16[2048,1024]{1,0:T(8,128)(2,1)}, u32[]{:S(2)}) copy-start(bf16[2048,1024]{1,0:T(8,128)(2,1)} %param.18) | copy-start | bytes 12582916
  218.3 105.4 %reduce-scatter.5.cloned.1.call-start = ((), (), s32[]{:S(2)}) async-start(), calls=%async_computation.6 | async-start | bytes 4456448 | tf_op jit(solution)/shard_map/reduce_scatter | solution.py:106
  250.8 116.3 %copy-start.5 = (f32[256,16]{0,1:T(8,128)S(1)}, f32[256,16]{0,1:T(8,128)}, u32[]{:S(2)}) copy-start(f32[256,16]{0,1:T(8,128)} %param.26) | copy-start | bytes 49156
  250.8 116.3 %copy-start.6 = (f32[256,16]{0,1:T(8,128)S(1)}, f32[256,16]{0,1:T(8,128)}, u32[]{:S(2)}) copy-start(f32[256,16]{0,1:T(8,128)} %param.27) | copy-start | bytes 49156
  250.8 116.9 %copy-start.1 = (f32[64,1024]{1,0:T(8,128)S(1)}, f32[64,1024]{1,0:T(8,128)}, u32[]{:S(2)}) copy-start(f32[64,1024]{1,0:T(8,128)} %param.22) | copy-start | bytes 786436
  250.8 116.9 %copy-start.2 = (f32[64,1024]{1,0:T(8,128)S(1)}, f32[64,1024]{1,0:T(8,128)}, u32[]{:S(2)}) copy-start(f32[64,1024]{1,0:T(8,128)} %param.23) | copy-start | bytes 786436
  250.8 116.9 %copy-start.3 = (f32[64,1024]{1,0:T(8,128)S(1)}, f32[64,1024]{1,0:T(8,128)}, u32[]{:S(2)}) copy-start(f32[64,1024]{1,0:T(8,128)} %param.24) | copy-start | bytes 786436
Sparse Core Ops, SparseCore 0:
  10.7 44.1 all-gather.3
  58.2 19.9 all-gather.5
  85.7 75.1 all-gather.7
  218.4 28.3 reduce-scatter.2
  250.9 72.7 reduce-scatter.4
where the time goes:
time: 379 us; the launch traced here: 378 us
  waiting for transfers between devices  174 us (46%)
  blocking collectives  128 us (34%)
  matrix products  47.1 us (12%)
  between operations  20.3 us (5%)
  other arithmetic  7.74 us (2%)
    reduce_scatter x1, waiting for transfers between devices, on_device(): lax.psum_scatter(jnp.einsum('td,th->dh', columns, first_grad, preferred_e...  59.8 us
    all_gather x1, waiting for transfers between devices, on_device(): lax.all_gather(hidden_weight.astype(jnp.bfloat16), 'blk', axis=0, tiled=T...  44.6 us
    psum x1, blocking collectives, on_device(): grad_total, resid_total = lax.psum((grad_part, resid_part), ('blk', 'feat'))  39.6 us
    psum x1, blocking collectives, on_device(): true_count = jnp.maximum(lax.psum(jnp.sum(keep_rows), 'blk'), 1.0)  34.6 us
    reduce_scatter x1, waiting for transfers between devices, on_device(): lax.psum_scatter(hidden_terms, 'feat', scatter_dimension=1, tiled=True)  28.4 us
    all_gather x1, waiting for transfers between devices, on_device(): lax.all_gather(features, 'blk', axis=0, tiled=True)  20.7 us
    all_gather x1, waiting for transfers between devices, on_device(): lax.all_gather(hidden, 'feat', axis=1, tiled=True)  20.1 us
    all_gather x1, blocking collectives, on_device(): lax.all_gather(resid_grad, 'blk', axis=0, tiled=True)  19.3 us
  transfers between devices with their start and end apart: 5, of which 5 were waited for; matrix products, arithmetic and copies ran while one was open for 2% of the time, Pallas kernels for 0%

commit v1 on v0

--- a/solution.py
+++ b/solution.py
@@ -13,6 +13,18 @@
 BETA_TWO = 0.999
 ADAM_EPS = 1e-08
 DECAY = 0.01
+
+
+def gather_by_bits(x, axis, dim):
+    ways, here = (lax.axis_size(axis), lax.axis_index(axis))
+    grown, reach = (x, 1)
+    while reach < ways:
+        theirs = lax.ppermute(grown, axis, [(d, d ^ reach) for d in range(ways)])
+        mine_first = jnp.concatenate([grown, theirs], axis=dim)
+        theirs_first = jnp.concatenate([theirs, grown], axis=dim)
+        grown = jnp.where(here & reach == 0, mine_first, theirs_first)
+        reach = 2 * reach
+    return grown
 
 
 def adamw_update(weight, moment, second, gradient, step_rate):
@@ -86,10 +98,7 @@
     residual = fitted - targets[:, None] - prior_draws
     resid_grad = (2.0 * keep_rows[:, None] * residual / (true_count * S)).astype(jnp.bfloat16)
     pulled_part, back_moments = fold_step(
-        (
-            lax.all_gather(features, "blk", axis=0, tiled=True),
-            lax.all_gather(resid_grad, "blk", axis=0, tiled=True),
-        )
+        (lax.all_gather(features, "blk", axis=0, tiled=True), gather_by_bits(resid_grad, "blk", 0))
     )
     alpha_grad = lax.psum(pulled_part, "feat") + NOISE * resid_grad.astype(jnp.float32)
     feature_grad = jnp.dot(resid_grad.astype(jnp.float32), moments.T, precision=PRECISE)

time: 379 us -> 373 us (0.984)
  blocking collectives: 128 us -> 108 us
  waiting for transfers between devices: 174 us -> 184 us
    all_gather x1 -> x0, blocking collectives: 19.3 us -> none  [on_device(): lax.all_gather(resid_grad, 'blk', axis=0, tiled=True)]
    ppermute x0 -> x4, waiting for transfers between devices: none -> 9.05 us  [gather_by_bits(): theirs = lax.ppermute(grown, axis, [(d, d ^ reach) for d in range(ways)])]
  transfers between devices with their start and end apart: 5 -> 9, of which waited for: 5 -> 8; matrix products, arithmetic and copies ran while one was open for 2% -> 4% of each run, Pallas kernels for 0% -> 0%
where the time goes in v1:
time: 373 us; the launch traced here: 372 us
  waiting for transfers between devices  184 us (49%)
  blocking collectives  108 us (29%)
  matrix products  46.9 us (13%)
  between operations  20.3 us (5%)
  other arithmetic  7.78 us (2%)
    reduce_scatter x1, waiting for transfers between devices, on_device(): lax.psum_scatter(jnp.einsum('td,th->dh', columns, first_grad, preferred_e...  59.8 us
    all_gather x1, waiting for transfers between devices, on_device(): lax.all_gather(hidden_weight.astype(jnp.bfloat16), 'blk', axis=0, tiled=T...  44.6 us
    psum x1, blocking collectives, on_device(): grad_total, resid_total = lax.psum((grad_part, resid_part), ('blk', 'feat'))  39.5 us
    psum x1, blocking collectives, on_device(): true_count = jnp.maximum(lax.psum(jnp.sum(keep_rows), 'blk'), 1.0)  34.6 us
    reduce_scatter x1, waiting for transfers between devices, on_device(): lax.psum_scatter(hidden_terms, 'feat', scatter_dimension=1, tiled=True)  29.7 us
    all_gather x1, waiting for transfers between devices, on_device(): lax.all_gather(features, 'blk', axis=0, tiled=True)  20.7 us
    all_gather x1, waiting for transfers between devices, on_device(): lax.all_gather(hidden, 'feat', axis=1, tiled=True)  20.1 us
    all_gather x1, blocking collectives, on_device(): lax.all_gather(alpha_low, 'blk', axis=0, tiled=True)  18.8 us
  transfers between devices with their start and end apart: 9, of which 8 were waited for; matrix products, arithmetic and copies ran while one was open for 4% of the time, Pallas kernels for 0%

profile of v1, /device:TPU:0, one launch (start us, length us, event | category | flops | bytes accessed | tf_op | source)
XLA Modules:
  0.0 372.0 jit_solution(7494557681231112278)
XLA Ops:
  7.2 0.0 copy-start.11
  7.2 0.0 all-gather.4.cloned.1.call-start
  7.2 1.6 convert_element_type.47
  8.9 0.0 all-gather.4.cloned.1.call-update
  8.9 0.0 all-gather.6.cloned.1.call-start
  8.9 1.4 fusion.3
  10.3 44.6 %all-gather.4.cloned.1.call-done = bf16[1024,1024]{1,0:T(8,128)(2,1)} async-done(((bf16[64,1024]{1,0:T(8,128)(2,1)}), bf16[1024,1024]{1,0:T(8,128)(2,1)}) %all-gather.4.cloned.1.call-update) | async-done | bytes 2097168 | tf_op jit(solution)/shard_map/all_gather | solution.py:74
  54.9 3.2 fusion.20
  58.1 0.0 all-gather.6.cloned.1.call-update
  58.1 0.0 copy-start.8
  58.1 0.0 copy-start.4
  58.1 0.0 all-gather.8.cloned.1.call-start
  58.2 20.1 %all-gather.6.cloned.1.call-done = bf16[256,2048]{1,0:T(8,128)(2,1)} async-done(((bf16[256,1024]{1,0:T(8,128)(2,1)}), bf16[256,2048]{1,0:T(8,128)(2,1)}) %all-gather.6.cloned.1.call-update) | async-done | bytes 1048592 | tf_op jit(solution)/shard_map/all_gather | solution.py:80
  78.3 0.0 copy-done.11
  78.3 7.3 %multiply_convert_fusion.1 = (bf16[256,1024]{1,0:T(8,128)(2,1)}, f32[256,1024]{1,0:T(8,128)S(1)}) fusion(f32[1024]{0:T(1024)S(1)} %copy-done.11, bf16[256,2048]{1,0:T(8,128)(2,1)} %all-gather.6.cloned.1.call-done, bf16[2048,1024]{1,0:T(8,128)(2,1)} %param.18), kind=kOutput, calls=%fused_computation.9 | convolution fusion | flops 1074528256 | bytes 6819840 | tf_op jit(solution)/shard_map/dot_general | solution.py:79
  85.6 0.0 all-gather.8.cloned.1.call-update
  85.6 0.0 reduce-scatter.3.cloned.1.call-start
  85.7 0.0 copy-done.8
  85.7 0.6 broadcast_multiply_fusion
  86.3 34.6 %psum.36 = f32[]{:T(128)} all-reduce(f32[]{:T(128)} %get-tuple-element.23), channel_id=1, replica_groups=mesh['blk'=16,'feat'=2] {'blk'}, use_global_device_ids=true, to_apply=%region_2.0 | all-reduce | flops 1 | bytes 8 | tf_op jit(solution)/shard_map/psum | solution.py:70
  120.9 0.0 copy-done.4
  121.5 18.8 %all_gather.16 = bf16[4096,16]{0,1:T(8,128)(2,1)S(1)} all-gather(bf16[256,16]{0,1:T(8,128)(2,1)S(1)} %convert_element_type.51), channel_id=1, replica_groups=mesh['blk'=16,'feat'=2] {'blk'}, dimensions={0}, use_global_device_ids=true | all-gather | bytes 139264 | tf_op jit(solution)/shard_map/all_gather | solution.py:94
  140.3 20.7 %all-gather.8.cloned.1.call-done = bf16[4096,1024]{1,0:T(8,128)(2,1)} async-done(((bf16[256,1024]{1,0:T(8,128)(2,1)}), bf16[4096,1024]{1,0:T(8,128)(2,1)}) %all-gather.8.cloned.1.call-update) | async-done | bytes 8388624 | tf_op jit(solution)/shard_map/all_gather | solution.py:93
  161.0 5.9 %fusion.21 = f32[256,4096]{1,0:T(8,128)S(1)} fusion(bf16[256,1024]{1,0:T(8,128)(2,1)} %get-tuple-element.26, bf16[4096,1024]{1,0:T(8,128)(2,1)} %all-gather.8.cloned.1.call-done), kind=kOutput, calls=%fused_computation.44 | convolution fusion | flops 2147483648 | bytes 13107200 | tf_op jit(solution)/shard_map/tf,pf->tp/dot_general | solution.py:40
  166.9 0.0 copy-start
  166.9 1.9 copy-done
  168.9 2.0 fusion.22
  170.9 8.3 %psum.35 = f32[256,16]{0,1:T(8,128)S(1)} all-reduce(f32[256,16]{0,1:T(8,128)S(1)} %fusion.22), channel_id=1, replica_groups=mesh['blk'=16,'feat'=2] {'feat'}, use_global_device_ids=true, to_apply=%region_0.0 | all-reduce | flops 4096 | bytes 32768 | tf_op jit(solution)/shard_map/psum | solution.py:97
  179.2 0.0 copy-done.7
  179.2 0.0 copy-done.9
  179.2 0.6 fusion.10
  179.8 0.0 collective-permute-start
  179.8 1.2 collective-permute-done
  181.0 0.1 collective-permute-start.1
  181.1 3.6 collective-permute-done.1
  184.8 1.5 collective-permute-start.2
  186.2 5.7 %fusion.23 = f32[1024,16]{1,0:T(8,128)S(1)} fusion(bf16[4096,1024]{1,0:T(8,128)(2,1)} %all-gather.8.cloned.1.call-done, bf16[4096,16]{0,1:T(8,128)(2,1)S(1)} %all_gather.16), kind=kOutput, calls=%fused_computation.46 | convolution fusion | flops 134217728 | bytes 8585216 | tf_op jit(solution)/shard_map/pf,ps->fs/dot_general | solution.py:42
  192.0 0.0 collective-permute-done.2
  192.0 1.0 collective-permute-start.3
  193.1 0.6 fusion.24
  193.7 0.0 copy-start.10
  193.7 4.2 %collective-permute-done.3 = bf16[2048,16]{0,1:T(8,128)(2,1)S(1)} collective-permute-done((bf16[2048,16]{0,1:T(8,128)(2,1)S(1)}, bf16[2048,16]{0,1:T(8,128)(2,1)S(1)}, u32[]{:S(2)}, u32[]{:S(2)}) %collective-permute-start.3) | collective-permute-done | bytes 65568 | tf_op jit(solution)/shard_map/ppermute | solution.py:22
  198.0 5.7 %fusion.9 = f32[1024,16]{1,0:T(8,128)S(1)} fusion(bf16[4096,1024]{1,0:T(8,128)(2,1)} %all-gather.8.cloned.1.call-done, bf16[2048,16]{0,1:T(8,128)(2,1)S(1)} %collective-permute-done.3, bf16[2048,16]{0,1:T(8,128)(2,1)S(1)} %maximum_select_fusion.1, pred[]{:T(512)S(6)} %eq.31), kind=kOutput, calls=%fused_computation.25 | convolution fusion | flops 134807552 | bytes 8585217 | tf_op jit(solution)/shard_map/pf,ps->fs/dot_general | solution.py:42
  203.7 4.3 %fusion.2 = bf16[256,1024]{1,0:T(8,128)(2,1)S(1)} fusion(f32[256,1024]{1,0:T(8,128)S(1)} %fusion.24, f32[1024,16]{1,0:T(8,128)S(1)} %fusion.9, bf16[256,16]{0,1:T(8,128)(2,1)S(1)} %convert_element_type.51, f32[256,1024]{1,0:T(8,128)S(1)} %get-tuple-element.27), kind=kOutput, calls=%fused_computation.5 | convolution fusion | flops 51380224 | bytes 2695168 | tf_op jit(solution)/shard_map/dot_general | solution.py:105
  208.0 0.0 copy-done.10
  208.0 2.6 fusion.25
  210.6 0.0 reduce-scatter.3.cloned.1.call-update
  210.6 0.0 reduce-scatter.5.cloned.1.call-start
  210.7 29.7 %reduce-scatter.3.cloned.1.call-done = f32[256,1024]{1,0:T(8,128)} async-done(((f32[256,2048]{1,0:T(8,128)}), f32[256,1024]{1,0:T(8,128)}) %reduce-scatter.3.cloned.1.call-update) | async-done | bytes 1048592 | tf_op jit(solution)/shard_map/reduce_scatter | solution.py:112
  240.4 3.9 %fusion.4 = f32[1024,1024]{1,0:T(8,128)} fusion(bf16[256,1024]{1,0:T(8,128)(2,1)S(1)} %fusion.3, f32[256,1024]{1,0:T(8,128)} %reduce-scatter.3.cloned.1.call-done, f32[256,1024]{1,0:T(8,128)S(1)} %get-tuple-element.25), kind=kOutput, calls=%fused_computation.10 | convolution fusion | flops 537919488 | bytes 6815744 | tf_op jit(solution)/shard_map/td,th->dh/dot_general | solution.py:116
  244.3 0.0 copy-start.3
  244.3 0.0 reduce-scatter.5.cloned.1.call-update
  245.1 4.2 %fusion.8 = f32[256,16]{0,1:T(8,128)S(1)} fusion(f32[256,4096]{1,0:T(8,128)} %copy-done, bf16[2048,16]{0,1:T(8,128)(2,1)S(1)} %collective-permute-done.3, bf16[2048,16]{0,1:T(8,128)(2,1)S(1)} %maximum_select_fusion.1, pred[]{:T(512)S(6)} %eq.31), kind=kOutput, calls=%fused_computation.24 | convolution fusion | flops 201916416 | bytes 4341761 | tf_op jit(solution)/shard_map/dot_general | solution.py:41
  249.3 7.0 %psum.37 = f32[256,16]{0,1:T(8,128)S(1)} all-reduce(f32[256,16]{0,1:T(8,128)S(1)} %fusion.8), channel_id=1, replica_groups=mesh['blk'=16,'feat'=2] {'feat'}, use_global_device_ids=true, to_apply=%region_6.7 | all-reduce | flops 4096 | bytes 32768 | tf_op jit(solution)/shard_map/psum | solution.py:103
  256.3 0.6 multiply_reduce_fusion.1
  257.5 59.8 %reduce-scatter.5.cloned.1.call-done = f32[64,1024]{1,0:T(8,128)} async-done(((f32[1024,1024]{1,0:T(8,128)}), f32[64,1024]{1,0:T(8,128)}) %reduce-scatter.5.cloned.1.call-update) | async-done | bytes 262160 | tf_op jit(solution)/shard_map/reduce_scatter | solution.py:115
  317.3 1.6 multiply_reduce_fusion
  319.6 39.5 %all-reduce = (f32[]{:T(128)}, f32[]{:T(128)}) all-reduce(f32[]{:T(128)S(6)} %add.72, f32[]{:T(128)S(6)} %mul.177), channel_id=1, replica_groups=mesh['blk'=16,'feat'=2] {'blk','feat'}, use_global_device_ids=true, to_apply=%region_8.9 | all-reduce | flops 2 | bytes 16 | tf_op jit(solution)/shard_map/psum | solution.py:124
  360.6 0.0 copy-done.5
  360.6 0.0 copy-done.6
  360.6 0.6 fusion.16
  361.2 0.0 copy-done.1
  361.2 0.0 copy-done.2
  361.2 2.0 fusion.18
  (13 shorter events, 0.1 us)
Async XLA Ops:
  7.2 71.1 %copy-start.11 = (f32[1024]{0:T(1024)S(1)}, f32[1024]{0:T(1024)}, u32[]{:S(2)}) copy-start(f32[1024]{0:T(1024)} %param.19) | copy-start | bytes 12292
  7.2 47.8 %all-gather.4.cloned.1.call-start = ((), (), s32[]{:S(2)}) async-start(), calls=%async_computation.2 | async-start | bytes 2228224 | tf_op jit(solution)/shard_map/all_gather | solution.py:74
  8.9 69.4 %all-gather.6.cloned.1.call-start = ((), (), s32[]{:S(2)}) async-start(), calls=%async_computation.3 | async-start | bytes 1572864 | tf_op jit(solution)/shard_map/all_gather | solution.py:80
  58.1 27.6 %copy-start.8 = (s32[256]{0:T(256)S(1)}, s32[256]{0:T(256)}, u32[]{:S(2)}) copy-start(s32[256]{0:T(256)} %param.16) | copy-start | bytes 3076
  58.1 62.7 %copy-start.4 = (f32[256,16]{0,1:T(8,128)S(1)}, f32[256,16]{0,1:T(8,128)}, u32[]{:S(2)}) copy-start(f32[256,16]{0,1:T(8,128)} %param.25) | copy-start | bytes 49156
  58.1 102.8 %all-gather.8.cloned.1.call-start = ((), (), s32[]{:S(2)}) async-start(), calls=%async_computation.4 | async-start | bytes 8912896 | tf_op jit(solution)/shard_map/all_gather | solution.py:93
  85.6 154.7 %reduce-scatter.3.cloned.1.call-start = ((), (), s32[]{:S(2)}) async-start(), calls=%async_computation.5 | async-start | bytes 3145728 | tf_op jit(solution)/shard_map/reduce_scatter | solution.py:112
  166.9 2.0 copy-start
  168.9 10.3 %copy-start.7 = (f32[256,16]{0,1:T(8,128)S(1)}, f32[256,16]{0,1:T(8,128)}, u32[]{:S(2)}) copy-start(f32[256,16]{0,1:T(8,128)} %param.21) | copy-start | bytes 49156
  168.9 10.3 %copy-start.9 = (f32[256]{0:T(256)S(1)}, f32[256]{0:T(256)}, u32[]{:S(2)}) copy-start(f32[256]{0:T(256)} %param.20) | copy-start | bytes 3076
  179.8 1.2 collective-permute-start
  181.0 3.7 %collective-permute-start.1 = (bf16[512,16]{0,1:T(8,128)(2,1)S(1)}, bf16[512,16]{0,1:T(8,128)(2,1)S(1)}, u32[]{:S(2)}, u32[]{:S(2)}) collective-permute-start(bf16[512,16]{0,1:T(8,128)(2,1)S(1)} %maximum_select_fusion.5), channel_id=1, source_target_pairs={{0,4},{2,6},{4,0},{6,2},{8,12},{10,14},{12,8},{14,10},{16,20},{18,... | collective-permute-start | bytes 49160 | tf_op jit(solution)/shard_map/ppermute | solution.py:22
  184.8 7.2 %collective-permute-start.2 = (bf16[1024,16]{0,1:T(8,128)(2,1)S(1)}, bf16[1024,16]{0,1:T(8,128)(2,1)S(1)}, u32[]{:S(2)}, u32[]{:S(2)}) collective-permute-start(bf16[1024,16]{0,1:T(8,128)(2,1)S(1)} %maximum_select_fusion.2), channel_id=1, source_target_pairs={{0,8},{2,10},{4,12},{6,14},{8,0},{10,2},{12,4},{14,6},{16,24},{18,... | collective-permute-start | bytes 98312 | tf_op jit(solution)/shard_map/ppermute | solution.py:22
  192.0 5.9 %collective-permute-start.3 = (bf16[2048,16]{0,1:T(8,128)(2,1)S(1)}, bf16[2048,16]{0,1:T(8,128)(2,1)S(1)}, u32[]{:S(2)}, u32[]{:S(2)}) collective-permute-start(bf16[2048,16]{0,1:T(8,128)(2,1)S(1)} %maximum_select_fusion.1), channel_id=1, source_target_pairs={{0,16},{2,18},{4,20},{6,22},{8,24},{10,26},{12,28},{14,30},{16,0},... | collective-permute-start | bytes 196616 | tf_op jit(solution)/shard_map/ppermute | solution.py:22
  193.7 14.3 %copy-start.10 = (bf16[2048,1024]{1,0:T(8,128)(2,1)S(1)}, bf16[2048,1024]{1,0:T(8,128)(2,1)}, u32[]{:S(2)}) copy-start(bf16[2048,1024]{1,0:T(8,128)(2,1)} %param.18) | copy-start | bytes 12582916
  210.6 106.7 %reduce-scatter.5.cloned.1.call-start = ((), (), s32[]{:S(2)}) async-start(), calls=%async_computation.6 | async-start | bytes 4456448 | tf_op jit(solution)/shard_map/reduce_scatter | solution.py:115
  244.3 116.3 %copy-start.5 = (f32[256,16]{0,1:T(8,128)S(1)}, f32[256,16]{0,1:T(8,128)}, u32[]{:S(2)}) copy-start(f32[256,16]{0,1:T(8,128)} %param.26) | copy-start | bytes 49156
  244.3 116.3 %copy-start.6 = (f32[256,16]{0,1:T(8,128)S(1)}, f32[256,16]{0,1:T(8,128)}, u32[]{:S(2)}) copy-start(f32[256,16]{0,1:T(8,128)} %param.27) | copy-start | bytes 49156
  244.3 116.9 %copy-start.1 = (f32[64,1024]{1,0:T(8,128)S(1)}, f32[64,1024]{1,0:T(8,128)}, u32[]{:S(2)}) copy-start(f32[64,1024]{1,0:T(8,128)} %param.22) | copy-start | bytes 786436
  244.3 116.9 %copy-start.2 = (f32[64,1024]{1,0:T(8,128)S(1)}, f32[64,1024]{1,0:T(8,128)}, u32[]{:S(2)}) copy-start(f32[64,1024]{1,0:T(8,128)} %param.23) | copy-start | bytes 786436
  244.3 116.9 %copy-start.3 = (f32[64,1024]{1,0:T(8,128)S(1)}, f32[64,1024]{1,0:T(8,128)}, u32[]{:S(2)}) copy-start(f32[64,1024]{1,0:T(8,128)} %param.24) | copy-start | bytes 786436
Sparse Core Ops, SparseCore 0:
  10.7 44.1 all-gather.3
  58.2 20.0 all-gather.5
  85.7 75.1 all-gather.7
  210.8 29.5 reduce-scatter.2
  244.5 72.8 reduce-scatter.4
